TPU v7x, 32 devices: a whole 2x2x4 slice. The times are simulated.
32 devices in a mesh: seq: 8 (over z, x), head: 4 (over y, core).
Axes of the slice: x: 2, y: 2, z: 4, core: 2. Of those that a mesh axis runs over, the one named last changes fastest.
Arguments:
- queries: bfloat16 [6144, 8192], P('seq', 'head'), may hold values from -6 to 6
- key_rows: bfloat16 [6144, 8192], P('seq', 'head'), may hold values from -0.5 to 0.5
- value_rows: bfloat16 [6144, 8192], P('seq', 'head'), may hold values from -130 to 130
- log_decay: float32 [64, 6144], P('head', 'seq'), may hold values from -1 to 0
- norm_gain: float32 [8192], P('head'), may hold values from 0.1 to 1.9
- grad_out: bfloat16 [6144, 8192], P('seq', 'head'), may hold values from -13 to 13
Outputs:
- output: bfloat16 [6144, 8192], P('seq', 'head')
- grad_queries: bfloat16 [6144, 8192], P('seq', 'head')
- grad_keys: bfloat16 [6144, 8192], P('seq', 'head')
- grad_values: bfloat16 [6144, 8192], P('seq', 'head')
- grad_gain: float32 [8192], P('head')
All inputs are finite; a program needn't handle non-finite values.
Results may differ from a plain program's by a relative error of at most 0.01.
Values sent between devices are 32-bit elements; how exact they have to be, the bound alone decides.
A program may use at most 192 MiB of HBM per device.

v0:
```python
import jax
import jax.numpy as jnp
from jax import lax
from jax.sharding import PartitionSpec as P

DH = 128
HD = 8192
EPSILON = 1e-06


def prefix(part, axis, combine, identity, reverse):
    count = lax.axis_size(axis)
    place = lax.axis_index(axis)
    ahead = count - 1 - place if reverse else place
    gathered = jax.tree.map(lambda a: lax.all_gather(a, axis), part)
    state = jax.tree.map(lambda a, e: jnp.zeros_like(a) + jnp.asarray(e, a.dtype), part, identity)

    def one(step, state):
        source = count - 1 - step if reverse else step
        return combine(
            state, jax.tree.map(lambda a: lax.dynamic_index_in_dim(a, source, 0, False), gathered)
        )

    return lax.fori_loop(0, ahead, one, state)


def split_pair(operand):
    high = operand.astype(jnp.bfloat16)
    low = (operand - high.astype(jnp.float32)).astype(jnp.bfloat16)
    return (high, low)


def split_product(form, left, right):
    if left.dtype == jnp.float32:
        high, low = split_pair(left)
        return jnp.einsum(form, high, right, preferred_element_type=jnp.float32) + jnp.einsum(
            form, low, right, preferred_element_type=jnp.float32
        )
    if right.dtype == jnp.float32:
        high, low = split_pair(right)
        return jnp.einsum(form, left, high, preferred_element_type=jnp.float32) + jnp.einsum(
            form, left, low, preferred_element_type=jnp.float32
        )
    return jnp.einsum(form, left, right, preferred_element_type=jnp.float32)


def causal_decay(cumulative):
    length = cumulative.shape[-1]
    below_diag = jnp.arange(length)[:, None] >= jnp.arange(length)[None, :]
    spread = cumulative[..., :, None] - cumulative[..., None, :]
    return jnp.where(below_diag, jnp.exp(jnp.where(below_diag, spread, 0.0)), 0.0)


def split_heads(matrix):
    return matrix.reshape(matrix.shape[0], -1, DH).transpose(1, 0, 2)


def merge_heads(tensor):
    return tensor.transpose(1, 0, 2).reshape(tensor.shape[1], -1)


def affine_combine(earlier, later):
    return (earlier[0] * later[0], later[0][:, None, None] * earlier[1] + later[1])


def intra_forward(operands):
    q_head, k_head, v_head, cumul = operands
    decay_mask = causal_decay(cumul)
    scores = jnp.dot(q_head, k_head.T, preferred_element_type=jnp.float32)
    weights = (scores * decay_mask).astype(jnp.bfloat16)
    return jnp.dot(weights, v_head, preferred_element_type=jnp.float32)


def intra_backward(operands):
    q_head, k_head, v_head, grad_head, cumul = operands
    decay_mask = causal_decay(cumul)
    scores = jnp.dot(q_head, k_head.T, preferred_element_type=jnp.float32)
    weights = (scores * decay_mask).astype(jnp.bfloat16)
    grad_scores = jnp.dot(grad_head, v_head.T, preferred_element_type=jnp.float32)
    grad_weights = (grad_scores * decay_mask).astype(jnp.bfloat16)
    grad_q = jnp.dot(grad_weights, k_head, preferred_element_type=jnp.float32)
    grad_k = jnp.dot(grad_weights.T, q_head, preferred_element_type=jnp.float32)
    grad_v = jnp.dot(weights.T, grad_head, preferred_element_type=jnp.float32)
    return (grad_q, grad_k, grad_v)


def on_device(queries, key_rows, value_rows, log_decay, norm_gain, grad_out):
    q_heads = split_heads(queries)
    k_heads = split_heads(key_rows)
    v_heads = split_heads(value_rows)
    cumulative = jnp.cumsum(log_decay, axis=1)
    block_total = cumulative[:, -1]
    growth = jnp.exp(cumulative)[..., None]
    tail = jnp.exp(block_total[:, None] - cumulative)[..., None]
    decay_total = jnp.exp(block_total)
    local_state = split_product("htd,hte->hde", k_heads * tail, v_heads)
    identity = (jnp.ones_like(decay_total), jnp.zeros_like(local_state))
    state_in = prefix((decay_total, local_state), "seq", affine_combine, identity, False)[1]
    intra = lax.map(intra_forward, (q_heads, k_heads, v_heads, cumulative))
    attended = intra + growth * split_product("htd,hde->hte", q_heads, state_in)
    mixed = merge_heads(attended)
    scaled_grad = grad_out.astype(jnp.float32) * norm_gain[None, :]
    square_sum = lax.psum(jnp.sum(mixed * mixed, axis=1), "head")
    inverse = lax.rsqrt(square_sum / HD + EPSILON)
    normed = mixed * inverse[:, None]
    inner_sum = lax.psum(jnp.sum(scaled_grad * normed, axis=1), "head")
    center = inner_sum / HD
    output = (normed * norm_gain[None, :]).astype(jnp.bfloat16)
    gain_part = jnp.sum(grad_out.astype(jnp.float32) * normed, axis=0)
    grad_gain = lax.psum(gain_part, "seq")
    grad_mixed = (inverse[:, None] * (scaled_grad - normed * center[:, None])).astype(jnp.bfloat16)
    grad_heads = split_heads(grad_mixed)
    state_grad = split_product("htd,hte->hde", q_heads * growth, grad_heads)
    identity = (jnp.ones_like(decay_total), jnp.zeros_like(state_grad))
    state_after = prefix((decay_total, state_grad), "seq", affine_combine, identity, True)[1]
    intra_q, intra_k, intra_v = lax.map(
        intra_backward, (q_heads, k_heads, v_heads, grad_heads, cumulative)
    )
    grad_q = intra_q + growth * split_product("hte,hde->htd", grad_heads, state_in)
    grad_k = intra_k + tail * split_product("hse,hde->hsd", v_heads, state_after)
    grad_v = intra_v + tail * split_product("hsd,hde->hse", k_heads, state_after)
    return (
        output,
        merge_heads(grad_q).astype(jnp.bfloat16),
        merge_heads(grad_k).astype(jnp.bfloat16),
        merge_heads(grad_v).astype(jnp.bfloat16),
        grad_gain,
    )


def solution(mesh):
    in_specs = (
        P("seq", "head"),
        P("seq", "head"),
        P("seq", "head"),
        P("head", "seq"),
        P("head"),
        P("seq", "head"),
    )
    out_specs = (P("seq", "head"), P("seq", "head"), P("seq", "head"), P("seq", "head"), P("head"))
    return jax.shard_map(
        on_device, mesh=mesh, in_specs=in_specs, out_specs=out_specs, check_vma=False
    )
```

profile of v0, /device:TPU:0, one launch (start us, length us, event | category | flops | bytes accessed | tf_op | source)
XLA Modules:
  0.0 436.8 jit_solution(12516096848934879581)
XLA Ops:
  12.4 4.7 %copy.68 = bf16[768,2048]{0,1:T(8,128)(2,1)} copy(bf16[768,2048]{1,0:T(8,128)(2,1)} %param.16) | data formatting | bytes 6291456 | tf_op args[2]
  25.3 4.6 %copy.71 = bf16[16,768,128]{2,1,0:T(8,128)(2,1)} copy(bf16[16,768,128]{1,2,0:T(8,128)(2,1)} %bitcast.184) | data formatting | bytes 6291456 | tf_op jit(solution)/shard_map/while | solution.py:99
  38.1 24.4 %all-reduce = f32[128]{0:T(128)S(1)} all-reduce(f32[128]{0:T(128)S(1)} %dynamic-update-slice), channel_id=2, replica_groups=mesh['seq'=8,'head'=4] {'seq'}, use_global_device_ids=true, to_apply=%add | all-reduce | flops 128 | bytes 1024
  62.6 3.4 broadcast.34.clone2
  65.9 45.5 %while.50 = (s32[]{:T(128)}, f32[16,768,128]{1,2,0:T(8,128)}, bf16[16,768,128]{2,1,0:T(8,128)(2,1)}, bf16[16,768,128]{2,1,0:T(8,128)(2,1)}, f32[16,768]{1,0:T(8,...) while((s32[]{:T(128)}, f32[16,768,128]{1,2,0:T(8,128)}, bf16[16,768,128]{2,1,0:T(8,128)(2,1)}, ...), condition=%wide.region_3.4_spmd, body=%wide.region_2.3_spmd.sunk | while | flops 305528832 | bytes 999513 | solution.py:99
  111.4 38.8 %all-gather.6.cloned.1.call-done = f32[128,128,128]{2,1,0:T(8,128)} async-done(((f32[16,128,128]{2,1,0:T(8,128)}), f32[128,128,128]{2,1,0:T(8,128)}) %all-gather.6.cloned.1.call-update) | async-done | bytes 8388624 | tf_op jit(solution)/shard_map/all_gather | solution.py:15
  155.0 4.4 fusion.59
  159.4 6.6 %copy.79 = f32[768,2048]{1,0:T(8,128)} copy(f32[768,2048]{0,1:T(8,128)} %bitcast.193) | data formatting | bytes 12582912 | tf_op jit(solution)/shard_map/reshape | solution.py:59
  165.9 5.8 %psum.21 = f32[768]{0:T(1024)S(1)} all-reduce(f32[768]{0:T(1024)S(1)} %get-tuple-element.338), channel_id=1, replica_groups=mesh['seq'=8,'head'=4] {'head'}, use_global_device_ids=true, to_apply=%region_7.8 | all-reduce | flops 768 | bytes 6144 | tf_op jit(solution)/shard_map/psum | solution.py:103
  171.8 4.8 %fusion.56 = (f32[2048]{0:T(1024)S(1)}, f32[768]{0:T(1024)S(1)}) fusion(bf16[768,2048]{1,0:T(8,128)(2,1)} %param.19, f32[768,2048]{1,0:T(8,128)} %copy.79, f32[768]{0:T(1024)S(1)} %add_rsqrt_fusion, f32[2048]{0:T(1024)S(1)} %copy-done.11), kind=kLoop, calls=%fused_computation.62 | loop fusion | flops 11007232 | bytes 9459712 | tf_op jit(solution)/shard_map/reduce_sum | solution.py:109
  176.6 6.4 %psum.22 = f32[768]{0:T(1024)S(1)} all-reduce(f32[768]{0:T(1024)S(1)} %get-tuple-element.281), channel_id=1, replica_groups=mesh['seq'=8,'head'=4] {'head'}, use_global_device_ids=true, to_apply=%region_9.10 | all-reduce | flops 768 | bytes 6144 | tf_op jit(solution)/shard_map/psum | solution.py:106
  183.0 5.9 %fusion.68 = (bf16[96,16,8,128]{3,2,1,0:T(8,128)(2,1)S(1)}, bf16[768,2048]{1,0:T(8,128)(2,1)}) fusion(f32[768,2048]{1,0:T(8,128)} %copy.79, bf16[768,2048]{1,0:T(8,128)(2,1)} %param.19, f32[768]{0:T(1024)S(1)} %broadcast_multiply_fusion, f32[2048]{0:T(1024)S(1)} %copy-done.11, f32[768]{0:T(1024)S(1)} %add_rsqrt_fusion), kind=kLoop, calls=%fused_computation.82 | loop fusion | flops 14155776 | bytes 15742976
  191.5 3.7 fusion.79
  201.8 3.3 broadcast.34.clone2.1
  208.3 137.7 %while.52 = (s32[]{:T(128)}, f32[16,768,128]{1,2,0:T(8,128)}, f32[16,768,128]{1,2,0:T(8,128)}, f32[16,768,128]{1,2,0:T(8,128)}, bf16[16,768,128]{2,1,0:T(8,128)(...) while((s32[]{:T(128)}, f32[16,768,128]{1,2,0:T(8,128)}, ...), condition=%wide.region_11.12_spmd, body=%wide.region_10.11_spmd.sunk | while | flops 762052608 | bytes 6122609 | solution.py:116
  346.1 8.5 %add_convert_fusion = bf16[16,768,128]{1,2,0:T(8,128)(2,1)} fusion(f32[16,768,128]{1,2,0:T(8,128)} %get-tuple-element.216, f32[16,768,128]{1,2,0:T(8,128)} %fusion.79, f32[16,768]{1,0:T(8,128)S(1)} %get-tuple-element.336, f32[16,128,128]{2,1,0:T(8,128)S(1)} %get-tuple-element.215, bf16[96,16,8,128]{3,2,1,0:T(8,128)(2,1)} %copy-done.9), kind=kOutput, calls=%fused_computation.73 | convolution fusion | flops 409993216 | bytes 19972096 | tf_op jit(solution)/shard_map/hte,hde->htd/dot_general | solution.py:41
  354.6 4.6 %copy.93 = bf16[768,2048]{1,0:T(8,128)(2,1)} copy(bf16[768,2048]{0,1:T(8,128)(2,1)} %bitcast.194) | data formatting | bytes 6291456
  359.2 30.1 %psum.23 = f32[2048]{0:T(1024)} all-reduce(f32[2048]{0:T(1024)S(1)} %get-tuple-element.280), channel_id=1, replica_groups=mesh['seq'=8,'head'=4] {'seq'}, use_global_device_ids=true, to_apply=%region_15.16 | all-reduce | flops 2048 | bytes 16384 | tf_op jit(solution)/shard_map/psum | solution.py:110
  389.4 10.7 %while.53 = (s32[]{:T(128)}, f32[16,128,128]{2,1,0:T(8,128)S(1)}, s32[]{:T(128)}, f32[8,16]{1,0:T(8,128)S(1)}, f32[8,16,128,128]{3,2,1,0:T(8,128)}, /*index=5*/s32[]{:T(128)}, s32[]{:T(128)}, s32[]{:T(128)}, s32[]{:T(128)}) while((s32[]{:T(128)}, f32[16,128,128]{2,1,0:T(8,128)S(1)}, s32[]{:T(128)}, f32[8,16]{1,0:T(8,128)S(1)}, ...), condition=%wide.region_13.14_spmd, body=%wide.region_12.13_spmd.sunk | while | flops 524294 | bytes 3146075 | solution.py:24
  403.1 3.7 fusion.75
  406.8 5.5 %fusion.58 = bf16[16,768,128]{1,2,0:T(8,128)(2,1)} fusion(f32[16,768,128]{1,2,0:T(8,128)} %get-tuple-element.217, f32[16,128,768]{2,1,0:T(8,128)S(1)} %fusion.77, f32[16,768]{1,0:T(8,128)S(1)} %get-tuple-element.337, bf16[16,768,128]{1,2,0:T(8,128)(2,1)S(1)} %bitcast.187, f32[16,128,128]{2,1,0:T(8,128)S(1)} %get-tuple-element.218), kind=kOutput, calls=%fused_computation.66 | convolution fusion | flops 409993216 | bytes 19972096 | tf_op jit(solution)/shard_map/hse,hde->hsd/dot_general | solution.py:41
  412.4 4.6 %copy.94 = bf16[768,2048]{1,0:T(8,128)(2,1)} copy(bf16[768,2048]{0,1:T(8,128)(2,1)} %bitcast.196) | data formatting | bytes 6291456
  417.0 8.3 %fusion.57 = bf16[16,768,128]{1,2,0:T(8,128)(2,1)} fusion(f32[16,768,128]{1,2,0:T(8,128)} %get-tuple-element.219, f32[16,128,768]{2,1,0:T(8,128)} %fusion.75, f32[16,768]{1,0:T(8,128)S(1)} %get-tuple-element.337, bf16[16,768,128]{1,2,0:T(8,128)(2,1)} %bitcast.181, f32[16,128,128]{2,1,0:T(8,128)S(1)} %get-tuple-element.218), kind=kOutput, calls=%fused_computation.64 | convolution fusion | flops 409993216 | bytes 19972096 | tf_op jit(solution)/shard_map/hsd,hde->hse/dot_general | solution.py:41
  425.3 4.6 %copy.95 = bf16[768,2048]{1,0:T(8,128)(2,1)} copy(bf16[768,2048]{0,1:T(8,128)(2,1)} %bitcast.195) | data formatting | bytes 6291456
  (186 shorter events, 234.3 us)
Async XLA Ops:
  7.2 3.3 copy-start
  7.2 143.0 %all-gather.6.cloned.1.call-start = ((), (), s32[]{:S(2)}) async-start(), calls=%async_computation | async-start | bytes 9437184 | tf_op jit(solution)/shard_map/all_gather | solution.py:15
  10.4 12.1 %copy-start.2 = (bf16[768,2048]{0,1:T(8,128)(2,1)}, bf16[768,2048]{0,1:T(8,128)(2,1)S(1)}, u32[]{:S(2)}) copy-start(bf16[768,2048]{0,1:T(8,128)(2,1)S(1)} %copy.65) | copy-start | bytes 9437188
  17.4 3.0 copy-start.4
  22.5 366.9 %all-gather.8.cloned.1.call-start = ((), (), s32[]{:S(2)}) async-start(), calls=%async_computation.1 | async-start | bytes 9437184 | tf_op jit(solution)/shard_map/all_gather | solution.py:15
  33.2 3.3 copy-start.6
  33.2 3.3 copy-start.12
  150.3 3.1 copy-start.7
  150.3 4.7 %copy-start.10 = (f32[16,768,128]{1,2,0:T(8,128)S(1)}, f32[16,768,128]{1,2,0:T(8,128)}, u32[]{:S(2)}) copy-start(f32[16,768,128]{1,2,0:T(8,128)} %get-tuple-element.214) | copy-start | bytes 18874372
  159.4 12.4 %copy-start.11 = (f32[2048]{0:T(1024)S(1)}, f32[2048]{0:T(1024)}, u32[]{:S(2)}) copy-start(f32[2048]{0:T(1024)} %param.18) | copy-start | bytes 24580
  188.9 7.4 %copy-start.9 = (bf16[96,16,8,128]{3,2,1,0:T(8,128)(2,1)}, bf16[96,16,8,128]{3,2,1,0:T(8,128)(2,1)S(1)}, u32[]{:S(2)}) copy-start(bf16[96,16,8,128]{3,2,1,0:T(8,128)(2,1)S(1)} %get-tuple-element.334) | copy-start | bytes 9437188
  191.5 3.7 copy-start.8
  400.1 3.0 copy-start.3
  403.1 3.7 copy-start.5
  425.3 4.6 %copy-start.1 = (f32[16,768]{1,0:T(8,128)S(1)}, f32[16,768]{1,0:T(8,128)}, u32[]{:S(2)}) copy-start(f32[16,768]{1,0:T(8,128)} %param.17) | copy-start | bytes 147460
Sparse Core Ops, SparseCore 0:
  22.6 127.5 all-gather.5
  198.7 132.5 all-gather.7
where the time goes:
time: 440 us; the launch traced here: 437 us
  matrix products  231 us (52%)
  blocking collectives  66.8 us (15%)
  local copies, waits for them, and re-layouts  61.9 us (14%)
  waiting for transfers between devices  38.8 us (9%)
  other arithmetic  22.7 us (5%)
  between operations  14.9 us (3%)
    dot_general x16, matrix products, intra_forward(): return jnp.dot(weights, v_head, preferred_element_type=jnp.float32)  45.1 us
    dot_general x16, matrix products, intra_backward(): grad_v = jnp.dot(weights.T, grad_head, preferred_element_type=jnp.float32)  44.1 us
    all_gather x2, waiting for transfers between devices, prefix(): gathered = jax.tree.map(lambda a: lax.all_gather(a, axis), part)  38.8 us
    dot_general x16, matrix products, intra_backward(): grad_q = jnp.dot(grad_weights, k_head, preferred_element_type=jnp.float32)  35.8 us
    dot_general x16, matrix products, intra_backward(): grad_k = jnp.dot(grad_weights.T, q_head, preferred_element_type=jnp.float32)  32.9 us
    psum x1, blocking collectives, on_device(): grad_gain = lax.psum(gain_part, 'seq')  30.1 us
    unnamed x35, local copies, waits for them, and re-layouts  27.5 us
    dot_general x4, matrix products, split_product(): jnp.einsum(form, left, low, preferred_element_type=jnp.float32)  26.7 us
  transfers between devices with their start and end apart: 2, of which 1 were waited for; matrix products, arithmetic and copies ran while one was open for 51% of the time, Pallas kernels for 0%

commit v1 on v0

--- a/solution.py
+++ b/solution.py
@@ -107,7 +107,19 @@
     center = inner_sum / HD
     output = (normed * norm_gain[None, :]).astype(jnp.bfloat16)
     gain_part = jnp.sum(grad_out.astype(jnp.float32) * normed, axis=0)
-    grad_gain = lax.psum(gain_part, "seq")
+
+    def part_notes(inputs):
+        base_arr = inputs
+        n_peers_all = lax.axis_size("seq")
+        for s in [it for it in (1, 2, 4, 8, 16) if it < n_peers_all]:
+            base_arr = base_arr + lax.ppermute(
+                base_arr,
+                axis_name="seq",
+                perm=list(map(lambda k0: (k0, k0 ^ s), range(n_peers_all))),
+            )
+        return base_arr
+
+    grad_gain = part_notes(gain_part)
     grad_mixed = (inverse[:, None] * (scaled_grad - normed * center[:, None])).astype(jnp.bfloat16)
     grad_heads = split_heads(grad_mixed)
     state_grad = split_product("htd,hte->hde", q_heads * growth, grad_heads)

time: 440 us -> 419 us (0.952)
  blocking collectives: 66.8 us -> 36.7 us
  starting transfers between devices: 0.08 us -> 13.6 us
  matrix products: 231 us -> 225 us
    psum x1 -> x0, blocking collectives: 30.1 us -> none  [on_device(): grad_gain = lax.psum(gain_part, 'seq')]
    ppermute x0 -> x3, starting transfers between devices: none -> 13.6 us  [part_notes(): lax.ppermute(base_arr, axis_name='seq', perm=list(map(lambda k0: (k0, k0...]
    dot_general x4, matrix products: 26.7 us -> 21.4 us  [split_product(): jnp.einsum(form, left, low, preferred_element_type=jnp.float32)]
    unnamed x35 -> x39, local copies, waits for them, and re-layouts: 27.5 us -> 29.3 us
  transfers between devices with their start and end apart: 2 -> 5, of which waited for: 1 -> 1; matrix products, arithmetic and copies ran while one was open for 51% -> 53% of each run, Pallas kernels for 0% -> 0%
where the time goes in v1:
time: 419 us; the launch traced here: 416 us
  matrix products  225 us (54%)
  local copies, waits for them, and re-layouts  63.5 us (15%)
  waiting for transfers between devices  38.9 us (9%)
  blocking collectives  36.7 us (9%)
  other arithmetic  23.3 us (6%)
  between operations  14.9 us (4%)
  starting transfers between devices  13.6 us (3%)
    dot_general x16, matrix products, intra_forward(): return jnp.dot(weights, v_head, preferred_element_type=jnp.float32)  45.1 us
    dot_general x16, matrix products, intra_backward(): grad_v = jnp.dot(weights.T, grad_head, preferred_element_type=jnp.float32)  43.9 us
    all_gather x2, waiting for transfers between devices, prefix(): gathered = jax.tree.map(lambda a: lax.all_gather(a, axis), part)  38.9 us
    dot_general x16, matrix products, intra_backward(): grad_q = jnp.dot(grad_weights, k_head, preferred_element_type=jnp.float32)  36 us
    dot_general x16, matrix products, intra_backward(): grad_k = jnp.dot(grad_weights.T, q_head, preferred_element_type=jnp.float32)  32.9 us
    unnamed x39, local copies, waits for them, and re-layouts  29.3 us
    dot_general x16, matrix products, intra_backward(): jnp.dot(grad_head, v_head.T, preferred_element_type=jnp.float32)  24.5 us
    unnamed x1, blocking collectives  24.4 us
  transfers between devices with their start and end apart: 5, of which 1 were waited for; matrix products, arithmetic and copies ran while one was open for 53% of the time, Pallas kernels for 0%

profile of v1, /device:TPU:0, one launch (start us, length us, event | category | flops | bytes accessed | tf_op | source)
XLA Modules:
  0.0 416.4 jit_solution(17420622956230175730)
XLA Ops:
  12.4 4.7 %copy.68 = bf16[768,2048]{0,1:T(8,128)(2,1)} copy(bf16[768,2048]{1,0:T(8,128)(2,1)} %param.16) | data formatting | bytes 6291456 | tf_op args[2]
  25.3 4.6 %copy.71 = bf16[16,768,128]{2,1,0:T(8,128)(2,1)} copy(bf16[16,768,128]{1,2,0:T(8,128)(2,1)} %bitcast.184) | data formatting | bytes 6291456 | tf_op jit(solution)/shard_map/while | solution.py:99
  30.0 3.3 copy.64
  37.9 24.4 %all-reduce = f32[128]{0:T(128)S(1)} all-reduce(f32[128]{0:T(128)S(1)} %dynamic-update-slice), channel_id=2, replica_groups=mesh['seq'=8,'head'=4] {'seq'}, use_global_device_ids=true, to_apply=%add | all-reduce | flops 128 | bytes 1024
  62.5 3.4 broadcast.34.clone2
  65.8 45.5 %while.50 = (s32[]{:T(128)}, f32[16,768,128]{1,2,0:T(8,128)}, bf16[16,768,128]{2,1,0:T(8,128)(2,1)}, bf16[16,768,128]{2,1,0:T(8,128)(2,1)}, f32[16,768]{1,0:T(8,...) while((s32[]{:T(128)}, f32[16,768,128]{1,2,0:T(8,128)}, bf16[16,768,128]{2,1,0:T(8,128)(2,1)}, ...), condition=%wide.region_3.4_spmd, body=%wide.region_2.3_spmd.sunk | while | flops 305528832 | bytes 999513 | solution.py:99
  111.3 38.9 %all-gather.6.cloned.1.call-done = f32[128,128,128]{2,1,0:T(8,128)} async-done(((f32[16,128,128]{2,1,0:T(8,128)}), f32[128,128,128]{2,1,0:T(8,128)}) %all-gather.6.cloned.1.call-update) | async-done | bytes 8388624 | tf_op jit(solution)/shard_map/all_gather | solution.py:15
  155.0 4.4 %fusion.59 = (f32[768]{0:T(1024)S(1)}, f32[16,768,128]{1,2,0:T(8,128)}) fusion(f32[16,768,128]{1,2,0:T(8,128)S(1)} %copy-done.12, f32[16,128,768]{2,1,0:T(8,128)S(1)} %fusion.81, bf16[16,768,128]{1,2,0:T(8,128)(2,1)S(1)} %bitcast.190, f32[16,128,128]{2,1,0:T(8,128)S(1)} %get-tuple-element.215, f32[16,768]{1,0:T(8,128)S(1)} %get-tuple-element.336), kind=kOutput, calls=%fused_computation.68 | convolution fusion | flops 411565312 | bytes 23120896 | tf_op jit(solution)/shard_map/htd,hde->hte/dot_general | solution.py:41
  159.4 6.6 %copy.79 = f32[768,2048]{1,0:T(8,128)} copy(f32[768,2048]{0,1:T(8,128)} %bitcast.193) | data formatting | bytes 12582912 | tf_op jit(solution)/shard_map/reshape | solution.py:59
  166.0 5.8 %psum.14 = f32[768]{0:T(1024)S(1)} all-reduce(f32[768]{0:T(1024)S(1)} %get-tuple-element.338), channel_id=1, replica_groups=mesh['seq'=8,'head'=4] {'head'}, use_global_device_ids=true, to_apply=%region_7.8 | all-reduce | flops 768 | bytes 6144 | tf_op jit(solution)/shard_map/psum | solution.py:103
  171.8 4.8 %fusion.56 = (f32[2048]{0:T(1024)S(1)}, f32[768]{0:T(1024)S(1)}) fusion(bf16[768,2048]{1,0:T(8,128)(2,1)} %param.19, f32[768,2048]{1,0:T(8,128)} %copy.79, f32[768]{0:T(1024)S(1)} %add_rsqrt_fusion, f32[2048]{0:T(1024)S(1)} %copy-done.13), kind=kLoop, calls=%fused_computation.62 | loop fusion | flops 11007232 | bytes 9459712 | tf_op jit(solution)/shard_map/reduce_sum | solution.py:109
  176.6 6.4 %psum.15 = f32[768]{0:T(1024)S(1)} all-reduce(f32[768]{0:T(1024)S(1)} %get-tuple-element.281), channel_id=1, replica_groups=mesh['seq'=8,'head'=4] {'head'}, use_global_device_ids=true, to_apply=%region_9.10 | all-reduce | flops 768 | bytes 6144 | tf_op jit(solution)/shard_map/psum | solution.py:106
  183.0 5.9 %fusion.68 = (bf16[96,16,8,128]{3,2,1,0:T(8,128)(2,1)S(1)}, bf16[768,2048]{1,0:T(8,128)(2,1)}) fusion(f32[768,2048]{1,0:T(8,128)} %copy.79, bf16[768,2048]{1,0:T(8,128)(2,1)} %param.19, f32[768]{0:T(1024)S(1)} %broadcast_multiply_fusion, f32[2048]{0:T(1024)S(1)} %copy-done.13, f32[768]{0:T(1024)S(1)} %add_rsqrt_fusion), kind=kLoop, calls=%fused_computation.82 | loop fusion | flops 14155776 | bytes 15742976
  198.4 3.4 broadcast.34.clone
  205.0 3.3 broadcast.34.clone2.2
  208.3 137.7 %while.52 = (s32[]{:T(128)}, f32[16,768,128]{1,2,0:T(8,128)}, f32[16,768,128]{1,2,0:T(8,128)}, f32[16,768,128]{1,2,0:T(8,128)}, bf16[16,768,128]{2,1,0:T(8,128)(...) while((s32[]{:T(128)}, f32[16,768,128]{1,2,0:T(8,128)}, ...), condition=%wide.region_11.12_spmd, body=%wide.region_10.11_spmd.sunk | while | flops 762052608 | bytes 6122609 | solution.py:128
  351.7 8.8 %collective-permute-start.2 = (f32[2048]{0:T(1024)S(1)}, f32[2048]{0:T(1024)S(1)}, u32[]{:S(2)}, u32[]{:S(2)}) collective-permute-start(f32[2048]{0:T(1024)S(1)} %add.110), channel_id=1, source_target_pairs={{0,16},{4,20},{8,24},{12,28},{16,0},{20,4},{24,8},{28,12},{1,17},{... | collective-permute-start | bytes 24584 | tf_op jit(solution)/shard_map/ppermute | solution.py:115
  363.7 4.6 %copy.93 = bf16[768,2048]{1,0:T(8,128)(2,1)} copy(bf16[768,2048]{0,1:T(8,128)(2,1)} %bitcast.194) | data formatting | bytes 6291456
  369.0 10.7 %while.53 = (s32[]{:T(128)}, f32[16,128,128]{2,1,0:T(8,128)S(1)}, s32[]{:T(128)}, f32[8,16]{1,0:T(8,128)S(1)}, f32[8,16,128,128]{3,2,1,0:T(8,128)}, /*index=5*/s32[]{:T(128)}, s32[]{:T(128)}, s32[]{:T(128)}, s32[]{:T(128)}) while((s32[]{:T(128)}, f32[16,128,128]{2,1,0:T(8,128)S(1)}, s32[]{:T(128)}, f32[8,16]{1,0:T(8,128)S(1)}, ...), condition=%wide.region_13.14_spmd, body=%wide.region_12.13_spmd.sunk | while | flops 524294 | bytes 3146075 | solution.py:24
  382.7 3.7 fusion.75
  386.4 5.5 %fusion.58 = bf16[16,768,128]{1,2,0:T(8,128)(2,1)} fusion(f32[16,768,128]{1,2,0:T(8,128)} %get-tuple-element.217, f32[16,128,768]{2,1,0:T(8,128)S(1)} %fusion.77, f32[16,768]{1,0:T(8,128)S(1)} %get-tuple-element.337, bf16[16,768,128]{1,2,0:T(8,128)(2,1)S(1)} %bitcast.187, f32[16,128,128]{2,1,0:T(8,128)S(1)} %get-tuple-element.218), kind=kOutput, calls=%fused_computation.66 | convolution fusion | flops 409993216 | bytes 19972096 | tf_op jit(solution)/shard_map/hse,hde->hsd/dot_general | solution.py:41
  392.0 4.6 %copy.94 = bf16[768,2048]{1,0:T(8,128)(2,1)} copy(bf16[768,2048]{0,1:T(8,128)(2,1)} %bitcast.196) | data formatting | bytes 6291456
  396.6 8.3 %fusion.57 = bf16[16,768,128]{1,2,0:T(8,128)(2,1)} fusion(f32[16,768,128]{1,2,0:T(8,128)} %get-tuple-element.219, f32[16,128,768]{2,1,0:T(8,128)} %fusion.75, f32[16,768]{1,0:T(8,128)S(1)} %get-tuple-element.337, bf16[16,768,128]{1,2,0:T(8,128)(2,1)} %bitcast.181, f32[16,128,128]{2,1,0:T(8,128)S(1)} %get-tuple-element.218), kind=kOutput, calls=%fused_computation.64 | convolution fusion | flops 409993216 | bytes 19972096 | tf_op jit(solution)/shard_map/hsd,hde->hse/dot_general | solution.py:41
  404.9 4.6 %copy.95 = bf16[768,2048]{1,0:T(8,128)(2,1)} copy(bf16[768,2048]{0,1:T(8,128)(2,1)} %bitcast.195) | data formatting | bytes 6291456
  (198 shorter events, 240.6 us)
Async XLA Ops:
  7.2 3.3 copy-start
  7.2 143.0 %all-gather.6.cloned.1.call-start = ((), (), s32[]{:S(2)}) async-start(), calls=%async_computation | async-start | bytes 9437184 | tf_op jit(solution)/shard_map/all_gather | solution.py:15
  10.4 12.1 %copy-start.2 = (bf16[768,2048]{0,1:T(8,128)(2,1)}, bf16[768,2048]{0,1:T(8,128)(2,1)S(1)}, u32[]{:S(2)}) copy-start(bf16[768,2048]{0,1:T(8,128)(2,1)S(1)} %copy.65) | copy-start | bytes 9437188
  17.4 3.0 copy-start.4
  22.5 346.4 %all-gather.8.cloned.1.call-start = ((), (), s32[]{:S(2)}) async-start(), calls=%async_computation.1 | async-start | bytes 9437184 | tf_op jit(solution)/shard_map/all_gather | solution.py:15
  33.3 3.2 copy-start.6
  33.3 3.2 copy-start.14
  150.3 3.1 copy-start.7
  150.3 4.7 %copy-start.12 = (f32[16,768,128]{1,2,0:T(8,128)S(1)}, f32[16,768,128]{1,2,0:T(8,128)}, u32[]{:S(2)}) copy-start(f32[16,768,128]{1,2,0:T(8,128)} %get-tuple-element.214) | copy-start | bytes 18874372
  159.4 12.4 %copy-start.13 = (f32[2048]{0:T(1024)S(1)}, f32[2048]{0:T(1024)}, u32[]{:S(2)}) copy-start(f32[2048]{0:T(1024)} %param.18) | copy-start | bytes 24580
  188.9 5.2 %copy-start.9 = (bf16[96,16,8,128]{3,2,1,0:T(8,128)(2,1)}, bf16[96,16,8,128]{3,2,1,0:T(8,128)(2,1)S(1)}, u32[]{:S(2)}) copy-start(bf16[96,16,8,128]{3,2,1,0:T(8,128)(2,1)S(1)} %get-tuple-element.334) | copy-start | bytes 9437188
  188.9 4.2 copy-start.8
  196.3 149.7 %collective-permute-start = (f32[2048]{0:T(1024)S(1)}, f32[2048]{0:T(1024)S(1)}, u32[]{:S(2)}, u32[]{:S(2)}) collective-permute-start(f32[2048]{0:T(1024)S(1)} %get-tuple-element.280), channel_id=1, source_target_pairs={{0,4},{4,0},{8,12},{12,8},{16,20},{20,16},{24,28},{28,24},{1,5},{5... | collective-permute-start | bytes 24584 | tf_op jit(solution)/shard_map/ppermute | solution.py:115
  346.1 14.5 %copy-start.10 = (bf16[96,16,8,128]{3,2,1,0:T(8,128)(2,1)S(1)}, bf16[96,16,8,128]{3,2,1,0:T(8,128)(2,1)}, u32[]{:S(2)}) copy-start(bf16[96,16,8,128]{3,2,1,0:T(8,128)(2,1)} %copy-done.9) | copy-start | bytes 9437188
  346.1 14.5 %copy-start.11 = (f32[16,768,128]{1,2,0:T(8,128)S(1)}, f32[16,768,128]{1,2,0:T(8,128)}, u32[]{:S(2)}) copy-start(f32[16,768,128]{1,2,0:T(8,128)} %get-tuple-element.216) | copy-start | bytes 18874372
  346.1 5.6 %collective-permute-start.1 = (f32[2048]{0:T(1024)S(1)}, f32[2048]{0:T(1024)S(1)}, u32[]{:S(2)}, u32[]{:S(2)}) collective-permute-start(f32[2048]{0:T(1024)S(1)} %add.109), channel_id=1, source_target_pairs={{0,8},{4,12},{8,0},{12,4},{16,24},{20,28},{24,16},{28,20},{1,9},{5... | collective-permute-start | bytes 24584 | tf_op jit(solution)/shard_map/ppermute | solution.py:115
  351.7 16.6 %collective-permute-start.2 = (f32[2048]{0:T(1024)S(1)}, f32[2048]{0:T(1024)S(1)}, u32[]{:S(2)}, u32[]{:S(2)}) collective-permute-start(f32[2048]{0:T(1024)S(1)} %add.110), channel_id=1, source_target_pairs={{0,16},{4,20},{8,24},{12,28},{16,0},{20,4},{24,8},{28,12},{1,17},{... | collective-permute-start | bytes 24584 | tf_op jit(solution)/shard_map/ppermute | solution.py:115
  379.7 3.0 copy-start.3
  382.7 3.7 copy-start.5
  404.9 4.6 %copy-start.1 = (f32[16,768]{1,0:T(8,128)S(1)}, f32[16,768]{1,0:T(8,128)}, u32[]{:S(2)}) copy-start(f32[16,768]{1,0:T(8,128)} %param.17) | copy-start | bytes 147460
Sparse Core Ops, SparseCore 0:
  22.6 127.5 all-gather.5
  196.5 132.5 all-gather.7
